TPU v7x, 256 devices: a whole 4x4x8 slice. The times are simulated.
256 devices in a mesh: rep: 16 (over z_lo, x), tp: 16 (over z_hi, y, core).
Axes of the slice: x: 4, y: 4, z: 8 (z_hi: 2, z_lo: 4; z = z_hi * 4 + z_lo), core: 2. Of those that a mesh axis runs over, the one named last changes fastest.
Arguments:
- tokens: bfloat16 [8192, 4096], P('rep'), may hold values from -6 to 6
- cotangent: bfloat16 [8192, 4096], P('rep'), may hold values from -6 to 6
- token_ids: int32 [8192], P('rep'), may hold values from 0 to 128255, as said below
- partner: int32 [16], replicated, may hold values from 0 to 15, as said below
- gate_up: bfloat16 [2, 4096, 14336], P(None, 'rep', 'tp'), may hold values from -0.09375 to 0.09375
- down: bfloat16 [14336, 4096], P('tp', 'rep'), may hold values from -0.046875 to 0.046875
- wide_side: float32 [16, 3, 64, 4096], P('rep', None, None, 'tp'), may hold values from -6 to 6
- hidden_side: float32 [16, 3, 64, 14336], P('rep', None, None, 'tp'), may hold values from -6 to 6
- wide_mom: float32 [16, 3, 64, 4096], P('rep', None, None, 'tp'), may hold values from -4 to 4
- hidden_mom: float32 [16, 3, 64, 14336], P('rep', None, None, 'tp'), may hold values from -4 to 4
- wide_var: float32 [16, 3, 64, 4096], P('rep', None, None, 'tp'), may hold values from 0.01 to 1
- hidden_var: float32 [16, 3, 64, 14336], P('rep', None, None, 'tp'), may hold values from 0.01 to 1
Outputs:
- new_wide: float32 [16, 3, 64, 4096], P('rep', None, None, 'tp')
- new_hidden: float32 [16, 3, 64, 14336], P('rep', None, None, 'tp')
- new_wide_mom: float32 [16, 3, 64, 4096], P('rep', None, None, 'tp')
- new_hidden_mom: float32 [16, 3, 64, 14336], P('rep', None, None, 'tp')
- new_wide_var: float32 [16, 3, 64, 4096], P('rep', None, None, 'tp')
- new_hidden_var: float32 [16, 3, 64, 14336], P('rep', None, None, 'tp')
- wide_copy: bfloat16 [16, 3, 64, 4096], P('rep')
Inputs may be any that keep to these rules, and one draw needn't show every extreme that they name: `token_ids`: in each replica's block of 512 positions the ids are nonzero up to that replica's length and 0 after it; lengths lie between 128 and 512, some replica has no padding and another has length 128. There is one k, 1 <= k < 16, such that partner[r] is r XOR k or r itself for every r; partner[partner[r]] = r.
All inputs are finite; a program needn't handle non-finite values.
Results may differ from a plain program's by a relative error of at most 0.014.
Values may be sent and summed in bfloat16 or wider, within the bound.
No kernel may reach another device: no remote copies, remote signals or barrier semaphores. Data moves between devices by JAX's collectives and lax.ppermute only.
A program may use at most 128 MiB of HBM per device.

v0:
```python
import math
import jax
import jax.numpy as jnp
from jax import lax
from jax.sharding import PartitionSpec as P

FF = 14336
adapter_scale = 0.5
learn_rate = 0.1
beta_one = 0.9
beta_two = 0.99
bias_one = 1.0 - 0.9**10
bias_two = 1.0 - 0.99**10
adam_eps = 1e-08


def partner_2(value, axis, distance):
    mask = 2**distance
    pairs = [(source, source ^ mask) for source in range(lax.axis_size(axis))]
    return lax.ppermute(value, axis, pairs)


def adam_step(param, moment, second, grad):
    moment_new = beta_one * moment + (1.0 - beta_one) * grad
    second_new = beta_two * second + (1.0 - beta_two) * grad * grad
    param_new = param - learn_rate * (moment_new / bias_one) / (
        jnp.sqrt(second_new / bias_two) + adam_eps
    )
    return (param_new, moment_new, second_new)


def contract_last(left, right):
    return lax.dot_general(
        left, right, (((1,), (1,)), ((), ())), preferred_element_type=jnp.float32
    )


def contract_leading(left, right):
    return lax.dot_general(
        left, right, (((0,), (0,)), ((), ())), preferred_element_type=jnp.float32
    )


def shards(
    tokens,
    cotangent,
    token_ids,
    partner,
    gate_up,
    down,
    wide_side,
    hidden_side,
    wide_mom,
    hidden_mom,
    wide_var,
    hidden_var,
):
    width = tokens.shape[1]
    adapter_rank = wide_side.shape[2]
    portion_weight = wide_side.shape[3]
    scale_left = 1.0 / math.sqrt(width)
    scale_right = 1.0 / math.sqrt(adapter_rank)
    scale_down = 1.0 / math.sqrt(FF)
    tp_index = lax.axis_index("tp")
    rep_index = lax.axis_index("rep")
    x_part = lax.dynamic_slice_in_dim(tokens, tp_index * portion_weight, portion_weight, 1)
    cols = tokens
    frozen_weights = jnp.einsum(
        "td,kdf->ktf",
        cols,
        lax.all_gather(gate_up, "rep", axis=1, tiled=True),
        preferred_element_type=jnp.float32,
    )
    wide = wide_side[0]
    hid = hidden_side[0]
    wide_b = wide.astype(jnp.bfloat16)
    hidden_right = hid.astype(jnp.bfloat16)
    pair_a = wide_b[:2].reshape(2 * adapter_rank, portion_weight)
    low_part = contract_last(x_part, pair_a)
    low = (lax.psum(low_part.astype(jnp.bfloat16), "tp").astype(jnp.float32) * scale_left).astype(
        jnp.bfloat16
    )
    gate_adapter_update = low[:, :adapter_rank]
    up_adapter_update = low[:, adapter_rank:]
    gate_values = frozen_weights[0] + adapter_scale * scale_right * jnp.dot(
        gate_adapter_update, hidden_right[0], preferred_element_type=jnp.float32
    )
    upper_bound = frozen_weights[1] + adapter_scale * scale_right * jnp.dot(
        up_adapter_update, hidden_right[1], preferred_element_type=jnp.float32
    )
    sig = jax.nn.sigmoid(gate_values)
    act = gate_values * sig
    hidden_state = (act * upper_bound).astype(jnp.bfloat16)
    live = token_ids != 0
    masked_values = jnp.where(live[:, None], cotangent, jnp.zeros_like(cotangent))
    masked_portion = lax.dynamic_slice_in_dim(
        masked_values, tp_index * portion_weight, portion_weight, 1
    )
    down_adapter_left = hidden_right[2]
    down_b = wide_b[2]
    ud_part = contract_last(hidden_state, down_adapter_left)
    w_part = contract_last(masked_portion, down_b)
    ud_sum, w_sum = lax.psum((ud_part, w_part), "tp")
    up_down_right = (ud_sum * scale_down).astype(jnp.bfloat16)
    weight_right = w_sum.astype(jnp.bfloat16)
    cols = masked_values
    hidden_gradient = contract_last(cols, lax.all_gather(down, "rep", axis=1, tiled=True))
    hidden_gradient = hidden_gradient + adapter_scale * scale_down * scale_right * jnp.dot(
        weight_right, down_adapter_left, preferred_element_type=jnp.float32
    )
    gate_gradient = (
        hidden_gradient * upper_bound * sig * (1.0 + gate_values * (1.0 - sig))
    ).astype(jnp.bfloat16)
    up_gradient = (hidden_gradient * act).astype(jnp.bfloat16)
    gradient_gate_right = (
        adapter_scale * scale_right * contract_leading(gate_adapter_update, gate_gradient)
    )
    gradient_up_right = (
        adapter_scale * scale_right * contract_leading(up_adapter_update, up_gradient)
    )
    gradient_down_left = (
        adapter_scale * scale_down * scale_right * contract_leading(weight_right, hidden_state)
    )
    gradient_down_right = (
        adapter_scale * scale_right * contract_leading(up_down_right, masked_portion)
    )
    activation_product = jnp.concatenate(
        [
            contract_last(gate_gradient, hidden_right[0]),
            contract_last(up_gradient, hidden_right[1]),
        ],
        axis=1,
    )
    full = lax.dot_general(
        activation_product,
        tokens.astype(jnp.float32),
        (((0,), (0,)), ((), ())),
        precision=lax.Precision.HIGHEST,
    )
    owned_slice = lax.psum_scatter(
        full.astype(jnp.bfloat16), "tp", scatter_dimension=1, tiled=True
    ).astype(jnp.float32)
    gradient_left = (
        adapter_scale
        * scale_left
        * scale_right
        * owned_slice.reshape(2, adapter_rank, portion_weight)
    )
    grad_wide = jnp.concatenate([gradient_left, gradient_down_right[None]], axis=0)
    grad_hid = jnp.stack([gradient_gate_right, gradient_up_right, gradient_down_left], axis=0)
    wide_new, wmom_new, wvar_new = adam_step(wide, wide_mom[0], wide_var[0], grad_wide)
    hid_new, hmom_new, hvar_new = adam_step(hid, hidden_mom[0], hidden_var[0], grad_hid)
    joined = jnp.concatenate([wide_new, hid_new], axis=2)
    own = jnp.arange(partner.shape[0], dtype=jnp.int32)
    shift_value = jnp.max(jnp.bitwise_xor(partner, own))
    received = joined
    for bit in range(lax.axis_size("rep").bit_length() - 1):
        swapped = partner_2(received.astype(jnp.bfloat16), "rep", bit).astype(received.dtype)
        received = jnp.where(
            jnp.bitwise_and(jnp.right_shift(shift_value, bit), 1) == 1, swapped, received
        )
    paired = partner[rep_index] != rep_index
    final = jnp.where(paired, 0.5 * (joined + received), joined)
    wide_final = final[:, :, :portion_weight]
    hid_final = final[:, :, portion_weight:]
    wide_copy = lax.all_gather(wide_final[None].astype(jnp.bfloat16), "tp", axis=3, tiled=True)
    return (
        wide_final[None],
        hid_final[None],
        wmom_new[None],
        hmom_new[None],
        wvar_new[None],
        hvar_new[None],
        wide_copy,
    )


def solution(mesh):
    return jax.shard_map(
        shards,
        mesh=mesh,
        in_specs=(
            P("rep", None),
            P("rep", None),
            P("rep"),
            P(),
            P(None, "rep", "tp"),
            P("tp", "rep"),
            P("rep", None, None, "tp"),
            P("rep", None, None, "tp"),
            P("rep", None, None, "tp"),
            P("rep", None, None, "tp"),
            P("rep", None, None, "tp"),
            P("rep", None, None, "tp"),
        ),
        out_specs=(
            P("rep", None, None, "tp"),
            P("rep", None, None, "tp"),
            P("rep", None, None, "tp"),
            P("rep", None, None, "tp"),
            P("rep", None, None, "tp"),
            P("rep", None, None, "tp"),
            P("rep", None, None, None),
        ),
        check_vma=False,
    )
```

profile of v0, /device:TPU:1, one launch (start us, length us, event | category | flops | bytes accessed | tf_op | source)
XLA Modules:
  0.0 716.5 jit_solution(17991723816460455682)
XLA Ops:
  8.1 1.0 bitcast_convert_fusion.1
  9.1 1.8 convolution_convert_fusion.1
  11.6 1.3 copy.19
  13.0 2.6 broadcast_select_fusion
  15.6 2.0 copy-done
  17.8 89.0 %all-reduce.7 = bf16[512,64]{0,1:T(8,128)(2,1)S(1)} all-reduce(f32[512,64]{0,1:T(8,128)S(1)} %fusion.24), channel_id=1, replica_groups=mesh['rep'=16,'tp'=16] {'tp'}, use_global_device_ids=true, to_apply=%region_0.0 | all-reduce | flops 32768 | bytes 196608 | tf_op jit(solution)/shard_map/psum | solution.py:103
  106.9 146.3 %all-reduce.4.cloned.1.call-done = bf16[512,128]{1,0:T(8,128)(2,1)} async-done(((bf16[512,128]{1,0:T(8,128)(2,1)}), bf16[512,128]{1,0:T(8,128)(2,1)}) %all-reduce.4.cloned.1.call-update) | async-done | bytes 131088 | tf_op jit(solution)/shard_map/psum | solution.py:80
  253.2 0.9 multiply_convert_fusion.4
  254.2 10.0 %fusion.50 = f32[512,896]{1,0:T(8,128)S(1)} fusion(bf16[512,4096]{1,0:T(8,128)(2,1)} %copy-done, bf16[896,4096]{1,0:T(8,128)(2,1)} %all-gather.5.cloned.1.call-done), kind=kOutput, calls=%fused_computation.93 | convolution fusion | flops 3758096384 | bytes 13369344 | tf_op jit(solution)/shard_map/dot_general | solution.py:33
  264.2 1.6 multiply_add_fusion
  265.9 43.2 %all-gather.7.cloned.1.call-done = bf16[2,4096,896]{1,2,0:T(8,128)(2,1)} async-done(((bf16[2,256,896]{1,2,0:T(8,128)(2,1)}), bf16[2,4096,896]{1,2,0:T(8,128)(2,1)}) %all-gather.7.cloned.1.call-update) | async-done | bytes 14680080 | tf_op jit(solution)/shard_map/all_gather | solution.py:71
  309.0 13.3 %fusion.2 = f32[2,512,896]{2,1,0:T(8,128)S(1)} fusion(bf16[2,4096,896]{1,2,0:T(8,128)(2,1)} %all-gather.7.cloned.1.call-done, bf16[512,4096]{1,0:T(8,128)(2,1)} %param.12), kind=kOutput, calls=%fused_computation.4 | convolution fusion | flops 7516192768 | bytes 22544384 | tf_op jit(solution)/shard_map/td,kdf->ktf/dot_general | solution.py:68
  322.8 1.0 copy-done.11
  323.9 2.2 multiply_convert_fusion.2
  326.1 2.0 fusion.39
  328.4 1.3 fusion.40
  329.7 1.3 fusion.41
  330.9 5.1 convolution_convert_fusion
  336.5 1.5 convolution_multiply_fusion.1
  339.5 174.8 %all-reduce.6.cloned.1.call-done = f32[512,64]{1,0:T(8,128)} async-done(((f32[512,64]{1,0:T(8,128)}), f32[512,64]{1,0:T(8,128)}) %all-reduce.6.cloned.1.call-update) | async-done | bytes 131088 | tf_op jit(solution)/shard_map/psum | solution.py:103
  514.4 1.2 convolution_multiply_fusion.3
  515.6 82.2 %reduce-scatter.2.cloned.1.call-done = bf16[128,256]{1,0:T(8,128)(2,1)} async-done(((bf16[128,4096]{1,0:T(8,128)(2,1)}), bf16[128,256]{1,0:T(8,128)(2,1)}) %reduce-scatter.2.cloned.1.call-update) | async-done | bytes 65552 | tf_op jit(solution)/shard_map/reduce_scatter | solution.py:140
  599.0 1.3 collective-permute-start
  601.5 6.2 collective-permute-done
  607.8 2.8 collective-permute-start.1
  611.2 8.5 %collective-permute-done.1 = bf16[3,64,1152]{2,1,0:T(8,128)(2,1)S(1)} collective-permute-done((bf16[3,64,1152]{2,1,0:T(8,128)(2,1)S(1)}, bf16[3,64,1152]{2,1,0:T(8,128)(2,1)S(1)}, u32[]{:S(2)}, u32[]{:S(2)}) %collective-permute-start.1) | collective-permute-done | bytes 442400 | tf_op jit(solution)/shard_map/ppermute | solution.py:20
  621.1 7.1 collective-permute-done.2
  630.7 20.2 %collective-permute-done.3 = bf16[3,64,1152]{2,1,0:T(8,128)(2,1)} collective-permute-done((bf16[3,64,1152]{2,1,0:T(8,128)(2,1)S(1)}, bf16[3,64,1152]{2,1,0:T(8,128)(2,1)}, u32[]{:S(2)}, u32[]{:S(2)}) %collective-permute-start.3) | collective-permute-done | bytes 442400 | tf_op jit(solution)/shard_map/ppermute | solution.py:20
  650.9 1.5 multiply_select_fusion
  653.1 2.7 fusion.14
  658.2 48.5 %all-gather.9.cloned.1.call-done = bf16[3,64,4096]{2,1,0:T(8,128)(2,1)} async-done(((bf16[3,64,256]{2,1,0:T(8,128)(2,1)}), bf16[3,64,4096]{2,1,0:T(8,128)(2,1)}) %all-gather.9.cloned.1.call-update) | async-done | bytes 1572880 | tf_op jit(solution)/shard_map/all_gather | solution.py:166
  706.6 2.7 copy.27
  (79 shorter events, 10.3 us)
Async XLA Ops:
  8.0 3.6 copy-start.13
  8.0 245.2 %all-reduce.4.cloned.1.call-start = ((), (), s32[]{:S(2)}) async-start(), calls=%async_computation.3 | async-start | bytes 262144 | tf_op jit(solution)/shard_map/psum | solution.py:80
  9.1 3.9 copy-start.21
  11.0 243.2 %all-gather.5.cloned.1.call-start = ((), (), s32[]{:S(2)}) async-start(), calls=%async_computation.1 | async-start | bytes 7798784 | tf_op jit(solution)/shard_map/all_gather | solution.py:107
  11.5 297.5 %all-gather.7.cloned.1.call-start = ((), (), s32[]{:S(2)}) async-start(), calls=%async_computation.2 | async-start | bytes 15597568 | tf_op jit(solution)/shard_map/all_gather | solution.py:71
  12.9 501.4 %all-reduce.6.cloned.1.call-start = ((), (), s32[]{:S(2)}) async-start(), calls=%async_computation.5 | async-start | bytes 524288 | tf_op jit(solution)/shard_map/psum | solution.py:103
  13.0 93.8 %copy-start.1 = (f32[1,3,64,896]{3,2,1,0:T(8,128)S(1)}, f32[1,3,64,896]{3,2,1,0:T(8,128)}, u32[]{:S(2)}) copy-start(f32[1,3,64,896]{3,2,1,0:T(8,128)} %param.19) | copy-start | bytes 2064388
  15.6 2.0 copy-start
  106.9 215.5 %copy-start.5 = (bf16[3,64,896]{2,1,0:T(8,128)(2,1)}, bf16[3,64,896]{2,1,0:T(8,128)(2,1)S(1)}, u32[]{:S(2)}) copy-start(bf16[3,64,896]{2,1,0:T(8,128)(2,1)S(1)} %bitcast_convert_fusion) | copy-start | bytes 1032196
  254.1 68.2 %copy-start.6 = (bf16[512,128]{1,0:T(8,128)(2,1)}, bf16[512,128]{1,0:T(8,128)(2,1)S(1)}, u32[]{:S(2)}) copy-start(bf16[512,128]{1,0:T(8,128)(2,1)S(1)} %multiply_convert_fusion.4) | copy-start | bytes 393220
  322.4 1.5 copy-start.11
  328.1 269.7 %reduce-scatter.2.cloned.1.call-start = ((), (), s32[]{:S(2)}) async-start(), calls=%async_computation.4 | async-start | bytes 1114112 | tf_op jit(solution)/shard_map/reduce_scatter | solution.py:140
  336.1 370.6 %all-gather.9.cloned.1.call-start = ((), (), s32[]{:S(2)}) async-start(), calls=%async_computation.6 | async-start | bytes 1671168 | tf_op jit(solution)/shard_map/all_gather | solution.py:166
  336.1 1.9 copy-start.7
  336.1 2.9 copy-start.2
  336.1 2.9 copy-start.4
  336.5 1.9 copy-start.8
  338.0 0.7 copy-start.9
  339.0 259.7 %copy-start.14 = (f32[1,3,64,256]{3,2,1,0:T(8,128)S(1)}, f32[1,3,64,256]{3,2,1,0:T(8,128)}, u32[]{:S(2)}) copy-start(f32[1,3,64,256]{3,2,1,0:T(8,128)} %param.18) | copy-start | bytes 589828
  339.0 259.7 %copy-start.15 = (f32[1,3,64,256]{3,2,1,0:T(8,128)S(1)}, f32[1,3,64,256]{3,2,1,0:T(8,128)}, u32[]{:S(2)}) copy-start(f32[1,3,64,256]{3,2,1,0:T(8,128)} %param.22) | copy-start | bytes 589828
  339.0 259.7 %copy-start.17 = (f32[1,3,64,256]{3,2,1,0:T(8,128)S(1)}, f32[1,3,64,256]{3,2,1,0:T(8,128)}, u32[]{:S(2)}) copy-start(f32[1,3,64,256]{3,2,1,0:T(8,128)} %param.20) | copy-start | bytes 589828
  339.5 260.7 %copy-start.22 = (s32[16]{0:T(128)S(1)}, s32[16]{0:T(128)}, u32[]{:S(2)}) copy-start(s32[16]{0:T(128)} %param.15) | copy-start | bytes 196
  515.6 83.3 %copy-start.19 = (f32[64,256]{1,0:T(8,128)}, f32[64,256]{1,0:T(8,128)S(1)}, u32[]{:S(2)}) copy-start(f32[64,256]{1,0:T(8,128)S(1)} %convolution_multiply_fusion.3) | copy-start | bytes 196612
  599.0 8.8 %collective-permute-start = (bf16[3,64,1152]{2,1,0:T(8,128)(2,1)S(1)}, bf16[3,64,1152]{2,1,0:T(8,128)(2,1)S(1)}, u32[]{:S(2)}, u32[]{:S(2)}) collective-permute-start(bf16[3,64,1152]{2,1,0:T(8,128)(2,1)S(1)} %fusion.18), channel_id=1, source_target_pairs={{0,16},{16,0},{32,48},{48,32},{64,80},{80,64},{96,112},{112,96},{1... | collective-permute-start | bytes 1327112 | tf_op jit(solution)/shard_map/ppermute | solution.py:20
  607.8 11.9 %collective-permute-start.1 = (bf16[3,64,1152]{2,1,0:T(8,128)(2,1)S(1)}, bf16[3,64,1152]{2,1,0:T(8,128)(2,1)S(1)}, u32[]{:S(2)}, u32[]{:S(2)}) collective-permute-start(bf16[3,64,1152]{2,1,0:T(8,128)(2,1)S(1)} %fusion.16), channel_id=1, source_target_pairs={{0,32},{16,48},{32,0},{48,16},{64,96},{80,112},{96,64},{112,80},{1... | collective-permute-start | bytes 1327112 | tf_op jit(solution)/shard_map/ppermute | solution.py:20
  619.9 8.3 %collective-permute-start.2 = (bf16[3,64,1152]{2,1,0:T(8,128)(2,1)S(1)}, bf16[3,64,1152]{2,1,0:T(8,128)(2,1)S(1)}, u32[]{:S(2)}, u32[]{:S(2)}) collective-permute-start(bf16[3,64,1152]{2,1,0:T(8,128)(2,1)S(1)} %fusion.49), channel_id=1, source_target_pairs={{0,64},{16,80},{32,96},{48,112},{64,0},{80,16},{96,32},{112,48},{1... | collective-permute-start | bytes 1327112 | tf_op jit(solution)/shard_map/ppermute | solution.py:20
  628.2 2.5 copy-start.12
  628.4 22.5 %collective-permute-start.3 = (bf16[3,64,1152]{2,1,0:T(8,128)(2,1)S(1)}, bf16[3,64,1152]{2,1,0:T(8,128)(2,1)}, u32[]{:S(2)}, u32[]{:S(2)}) collective-permute-start(bf16[3,64,1152]{2,1,0:T(8,128)(2,1)S(1)} %fusion.17), channel_id=1, source_target_pairs={{0,128},{16,144},{32,160},{48,176},{64,192},{80,208},{96,224},{112... | collective-permute-start | bytes 1327112 | tf_op jit(solution)/shard_map/ppermute | solution.py:20
  630.7 22.4 %copy-start.3 = (f32[1,3,64,896]{3,2,1,0:T(8,128)S(1)}, f32[1,3,64,896]{3,2,1,0:T(8,128)}, u32[]{:S(2)}) copy-start(f32[1,3,64,896]{3,2,1,0:T(8,128)} %param.23) | copy-start | bytes 2064388
  652.3 3.4 copy-start.16
  652.3 3.4 copy-start.18
  652.4 3.4 copy-start.20
  (1 other events, 0.7 us)
Sparse Core Ops, SparseCore 0:
  12.0 241.1 all-reduce.3
  328.2 186.0 all-reduce.5
  519.1 78.7 reduce-scatter.1
  653.2 53.4 all-gather.8
Sparse Core Ops, SparseCore 1:
  13.2 110.5 all-gather.4
  125.9 183.0 all-gather.6
where the time goes:
time: 717 us; the launch traced here: 716 us
  waiting for transfers between devices  538 us (75%)
  blocking collectives  89 us (12%)
  matrix products  42.7 us (6%)
  between operations  18.9 us (3%)
  other arithmetic  12.1 us (2%)
  local copies, waits for them, and re-layouts  10.7 us (1%)
    psum x1, waiting for transfers between devices, shards(): ud_sum, w_sum = lax.psum((ud_part, w_part), 'tp')  175 us
    psum x1, waiting for transfers between devices, shards(): lax.psum(low_part.astype(jnp.bfloat16), 'tp').astype(jnp.float32)  146 us
    psum x1, blocking collectives, shards(): ud_sum, w_sum = lax.psum((ud_part, w_part), 'tp')  89 us
    reduce_scatter x1, waiting for transfers between devices, shards(): lax.psum_scatter(full.astype(jnp.bfloat16), 'tp', scatter_dimension=1, ti...  82.2 us
    all_gather x1, waiting for transfers between devices, shards(): lax.all_gather(wide_final[None].astype(jnp.bfloat16), 'tp', axis=3, tiled...  48.5 us
    all_gather x1, waiting for transfers between devices, shards(): lax.all_gather(gate_up, 'rep', axis=1, tiled=True)  43.2 us
    ppermute x4, waiting for transfers between devices, partner_2(): return lax.ppermute(value, axis, pairs)  42 us
    dot_general x6, matrix products, contract_last(): lax.dot_general(left, right, (((1,), (1,)), ((), ())), preferred_element_...  16.6 us
  transfers between devices with their start and end apart: 10, of which 9 were waited for; matrix products, arithmetic and copies ran while one was open for 5% of the time, Pallas kernels for 0%

commit v1 on v0

--- a/solution.py
+++ b/solution.py
@@ -77,9 +77,10 @@
     hidden_right = hid.astype(jnp.bfloat16)
     pair_a = wide_b[:2].reshape(2 * adapter_rank, portion_weight)
     low_part = contract_last(x_part, pair_a)
-    low = (lax.psum(low_part.astype(jnp.bfloat16), "tp").astype(jnp.float32) * scale_left).astype(
-        jnp.bfloat16
-    )
+    low = (
+        jnp.sum(lax.all_gather(low_part.astype(jnp.bfloat16), "tp"), axis=0).astype(jnp.float32)
+        * scale_left
+    ).astype(jnp.bfloat16)
     gate_adapter_update = low[:, :adapter_rank]
     up_adapter_update = low[:, adapter_rank:]
     gate_values = frozen_weights[0] + adapter_scale * scale_right * jnp.dot(

time: 717 us -> 775 us (1.081)
  waiting for transfers between devices: 538 us -> 596 us
    psum x1 -> x0, waiting for transfers between devices: 146 us -> none  [shards(): lax.psum(low_part.astype(jnp.bfloat16), 'tp').astype(jnp.float32)]
    all_gather x1, waiting for transfers between devices: 43.2 us -> 176 us  [shards(): lax.all_gather(gate_up, 'rep', axis=1, tiled=True)]
    all_gather x1, waiting for transfers between devices: 0.03 us -> 71.3 us  [shards(): lax.all_gather(down, 'rep', axis=1, tiled=True)]
where the time goes in v1:
time: 775 us; the launch traced here: 774 us
  waiting for transfers between devices  596 us (77%)
  blocking collectives  88.5 us (11%)
  matrix products  42.6 us (5%)
  between operations  17.8 us (2%)
  other arithmetic  13.3 us (2%)
  local copies, waits for them, and re-layouts  10.7 us (1%)
    all_gather x1, waiting for transfers between devices, shards(): lax.all_gather(gate_up, 'rep', axis=1, tiled=True)  176 us
    psum x1, waiting for transfers between devices, shards(): ud_sum, w_sum = lax.psum((ud_part, w_part), 'tp')  175 us
    psum x1, blocking collectives, shards(): ud_sum, w_sum = lax.psum((ud_part, w_part), 'tp')  88.5 us
    reduce_scatter x1, waiting for transfers between devices, shards(): lax.psum_scatter(full.astype(jnp.bfloat16), 'tp', scatter_dimension=1, ti...  82.1 us
    all_gather x1, waiting for transfers between devices, shards(): lax.all_gather(down, 'rep', axis=1, tiled=True)  71.3 us
    all_gather x1, waiting for transfers between devices, shards(): lax.all_gather(wide_final[None].astype(jnp.bfloat16), 'tp', axis=3, tiled...  48.5 us
    ppermute x4, waiting for transfers between devices, partner_2(): return lax.ppermute(value, axis, pairs)  41.8 us
    dot_general x6, matrix products, contract_last(): lax.dot_general(left, right, (((1,), (1,)), ((), ())), preferred_element_...  16.5 us
  transfers between devices with their start and end apart: 10, of which 9 were waited for; matrix products, arithmetic and copies ran while one was open for 5% of the time, Pallas kernels for 0%

profile of v1, /device:TPU:1, one launch (start us, length us, event | category | flops | bytes accessed | tf_op | source)
XLA Modules:
  0.0 774.2 jit_solution(14353972697359689238)
XLA Ops:
  7.2 1.0 bitcast_convert_fusion.1
  8.3 1.8 convolution_convert_fusion.1
  10.9 1.3 copy.19
  12.3 2.6 broadcast_select_fusion
  15.0 2.0 copy-done
  17.2 88.5 %all-reduce.4 = bf16[512,64]{0,1:T(8,128)(2,1)S(1)} all-reduce(f32[512,64]{0,1:T(8,128)S(1)} %fusion.24), channel_id=1, replica_groups=mesh['rep'=16,'tp'=16] {'tp'}, use_global_device_ids=true, to_apply=%region_0.0 | all-reduce | flops 32768 | bytes 196608 | tf_op jit(solution)/shard_map/psum | solution.py:104
  105.7 2.0 reduce_sum.12
  107.8 71.3 %all-gather.7.cloned.1.call-done = bf16[896,4096]{1,0:T(8,128)(2,1)} async-done(((bf16[896,256]{1,0:T(8,128)(2,1)}), bf16[896,4096]{1,0:T(8,128)(2,1)}) %all-gather.7.cloned.1.call-update) | async-done | bytes 7340048 | tf_op jit(solution)/shard_map/all_gather | solution.py:108
  179.1 9.9 %fusion.50 = f32[512,896]{1,0:T(8,128)S(1)} fusion(bf16[512,4096]{1,0:T(8,128)(2,1)} %copy-done, bf16[896,4096]{1,0:T(8,128)(2,1)} %all-gather.7.cloned.1.call-done), kind=kOutput, calls=%fused_computation.93 | convolution fusion | flops 3758096384 | bytes 13369344 | tf_op jit(solution)/shard_map/dot_general | solution.py:33
  189.0 1.6 multiply_add_fusion
  190.7 175.9 %all-gather.9.cloned.1.call-done = bf16[2,4096,896]{1,2,0:T(8,128)(2,1)} async-done(((bf16[2,256,896]{1,2,0:T(8,128)(2,1)}), bf16[2,4096,896]{1,2,0:T(8,128)(2,1)}) %all-gather.9.cloned.1.call-update) | async-done | bytes 14680080 | tf_op jit(solution)/shard_map/all_gather | solution.py:71
  366.6 13.3 %fusion.2 = f32[2,512,896]{2,1,0:T(8,128)S(1)} fusion(bf16[2,4096,896]{1,2,0:T(8,128)(2,1)} %all-gather.9.cloned.1.call-done, bf16[512,4096]{1,0:T(8,128)(2,1)} %param.12), kind=kOutput, calls=%fused_computation.4 | convolution fusion | flops 7516192768 | bytes 22544384 | tf_op jit(solution)/shard_map/td,kdf->ktf/dot_general | solution.py:68
  380.4 1.0 copy-done.11
  381.5 2.2 multiply_convert_fusion.2
  383.7 2.0 fusion.39
  385.9 1.3 fusion.40
  387.2 1.3 fusion.41
  388.5 5.1 convolution_convert_fusion
  394.1 1.5 convolution_multiply_fusion.1
  397.1 175.4 %all-reduce.3.cloned.1.call-done = f32[512,64]{1,0:T(8,128)} async-done(((f32[512,64]{1,0:T(8,128)}), f32[512,64]{1,0:T(8,128)}) %all-reduce.3.cloned.1.call-update) | async-done | bytes 131088 | tf_op jit(solution)/shard_map/psum | solution.py:104
  572.5 1.2 convolution_multiply_fusion.3
  573.8 82.1 %reduce-scatter.2.cloned.1.call-done = bf16[128,256]{1,0:T(8,128)(2,1)} async-done(((bf16[128,4096]{1,0:T(8,128)(2,1)}), bf16[128,256]{1,0:T(8,128)(2,1)}) %reduce-scatter.2.cloned.1.call-update) | async-done | bytes 65552 | tf_op jit(solution)/shard_map/reduce_scatter | solution.py:141
  657.0 1.3 collective-permute-start
  659.5 6.2 collective-permute-done
  665.8 2.8 collective-permute-start.1
  669.2 8.5 %collective-permute-done.1 = bf16[3,64,1152]{2,1,0:T(8,128)(2,1)S(1)} collective-permute-done((bf16[3,64,1152]{2,1,0:T(8,128)(2,1)S(1)}, bf16[3,64,1152]{2,1,0:T(8,128)(2,1)S(1)}, u32[]{:S(2)}, u32[]{:S(2)}) %collective-permute-start.1) | collective-permute-done | bytes 442400 | tf_op jit(solution)/shard_map/ppermute | solution.py:20
  679.1 7.1 collective-permute-done.2
  688.7 20.1 %collective-permute-done.3 = bf16[3,64,1152]{2,1,0:T(8,128)(2,1)} collective-permute-done((bf16[3,64,1152]{2,1,0:T(8,128)(2,1)S(1)}, bf16[3,64,1152]{2,1,0:T(8,128)(2,1)}, u32[]{:S(2)}, u32[]{:S(2)}) %collective-permute-start.3) | collective-permute-done | bytes 442400 | tf_op jit(solution)/shard_map/ppermute | solution.py:20
  708.8 1.5 multiply_select_fusion
  711.0 2.7 fusion.14
  716.1 48.5 %all-gather.13.cloned.1.call-done = bf16[3,64,4096]{2,1,0:T(8,128)(2,1)} async-done(((bf16[3,64,256]{2,1,0:T(8,128)(2,1)}), bf16[3,64,4096]{2,1,0:T(8,128)(2,1)}) %all-gather.13.cloned.1.call-update) | async-done | bytes 1572880 | tf_op jit(solution)/shard_map/all_gather | solution.py:167
  764.6 2.7 copy.26
  (80 shorter events, 10.6 us)
Async XLA Ops:
  7.2 3.8 copy-start.13
  7.2 98.6 %all-gather.11.cloned.1.call-start = ((), (), s32[]{:S(2)}) async-start(), calls=%async_computation.5 | async-start | bytes 2228224 | tf_op jit(solution)/shard_map/all_gather | solution.py:81
  8.3 4.1 copy-start.21
  10.1 169.0 %all-gather.7.cloned.1.call-start = ((), (), s32[]{:S(2)}) async-start(), calls=%async_computation.1 | async-start | bytes 7798784 | tf_op jit(solution)/shard_map/all_gather | solution.py:108
  10.9 355.7 %all-gather.9.cloned.1.call-start = ((), (), s32[]{:S(2)}) async-start(), calls=%async_computation.2 | async-start | bytes 15597568 | tf_op jit(solution)/shard_map/all_gather | solution.py:71
  12.3 560.3 %all-reduce.3.cloned.1.call-start = ((), (), s32[]{:S(2)}) async-start(), calls=%async_computation.4 | async-start | bytes 524288 | tf_op jit(solution)/shard_map/psum | solution.py:104
  12.3 93.3 %copy-start.1 = (f32[1,3,64,896]{3,2,1,0:T(8,128)S(1)}, f32[1,3,64,896]{3,2,1,0:T(8,128)}, u32[]{:S(2)}) copy-start(f32[1,3,64,896]{3,2,1,0:T(8,128)} %param.19) | copy-start | bytes 2064388
  14.9 2.0 copy-start
  105.7 274.3 %copy-start.5 = (bf16[3,64,896]{2,1,0:T(8,128)(2,1)}, bf16[3,64,896]{2,1,0:T(8,128)(2,1)S(1)}, u32[]{:S(2)}) copy-start(bf16[3,64,896]{2,1,0:T(8,128)(2,1)S(1)} %bitcast_convert_fusion) | copy-start | bytes 1032196
  107.8 272.2 %copy-start.6 = (bf16[512,128]{1,0:T(8,128)(2,1)}, bf16[512,128]{1,0:T(8,128)(2,1)S(1)}, u32[]{:S(2)}) copy-start(bf16[512,128]{1,0:T(8,128)(2,1)S(1)} %multiply_convert_fusion.4) | copy-start | bytes 393220
  380.0 1.5 copy-start.11
  385.7 270.1 %reduce-scatter.2.cloned.1.call-start = ((), (), s32[]{:S(2)}) async-start(), calls=%async_computation.3 | async-start | bytes 1114112 | tf_op jit(solution)/shard_map/reduce_scatter | solution.py:141
  393.7 371.0 %all-gather.13.cloned.1.call-start = ((), (), s32[]{:S(2)}) async-start(), calls=%async_computation.6 | async-start | bytes 1671168 | tf_op jit(solution)/shard_map/all_gather | solution.py:167
  393.7 1.9 copy-start.7
  393.7 2.9 copy-start.2
  393.7 2.9 copy-start.4
  394.0 1.9 copy-start.8
  395.6 0.7 copy-start.9
  396.6 260.1 %copy-start.14 = (f32[1,3,64,256]{3,2,1,0:T(8,128)S(1)}, f32[1,3,64,256]{3,2,1,0:T(8,128)}, u32[]{:S(2)}) copy-start(f32[1,3,64,256]{3,2,1,0:T(8,128)} %param.18) | copy-start | bytes 589828
  396.6 260.1 %copy-start.15 = (f32[1,3,64,256]{3,2,1,0:T(8,128)S(1)}, f32[1,3,64,256]{3,2,1,0:T(8,128)}, u32[]{:S(2)}) copy-start(f32[1,3,64,256]{3,2,1,0:T(8,128)} %param.22) | copy-start | bytes 589828
  396.6 260.1 %copy-start.17 = (f32[1,3,64,256]{3,2,1,0:T(8,128)S(1)}, f32[1,3,64,256]{3,2,1,0:T(8,128)}, u32[]{:S(2)}) copy-start(f32[1,3,64,256]{3,2,1,0:T(8,128)} %param.20) | copy-start | bytes 589828
  397.1 261.1 %copy-start.22 = (s32[16]{0:T(128)S(1)}, s32[16]{0:T(128)}, u32[]{:S(2)}) copy-start(s32[16]{0:T(128)} %param.15) | copy-start | bytes 196
  573.8 83.1 %copy-start.19 = (f32[64,256]{1,0:T(8,128)}, f32[64,256]{1,0:T(8,128)S(1)}, u32[]{:S(2)}) copy-start(f32[64,256]{1,0:T(8,128)S(1)} %convolution_multiply_fusion.3) | copy-start | bytes 196612
  657.0 8.8 %collective-permute-start = (bf16[3,64,1152]{2,1,0:T(8,128)(2,1)S(1)}, bf16[3,64,1152]{2,1,0:T(8,128)(2,1)S(1)}, u32[]{:S(2)}, u32[]{:S(2)}) collective-permute-start(bf16[3,64,1152]{2,1,0:T(8,128)(2,1)S(1)} %fusion.18), channel_id=1, source_target_pairs={{0,16},{16,0},{32,48},{48,32},{64,80},{80,64},{96,112},{112,96},{1... | collective-permute-start | bytes 1327112 | tf_op jit(solution)/shard_map/ppermute | solution.py:20
  665.8 11.9 %collective-permute-start.1 = (bf16[3,64,1152]{2,1,0:T(8,128)(2,1)S(1)}, bf16[3,64,1152]{2,1,0:T(8,128)(2,1)S(1)}, u32[]{:S(2)}, u32[]{:S(2)}) collective-permute-start(bf16[3,64,1152]{2,1,0:T(8,128)(2,1)S(1)} %fusion.16), channel_id=1, source_target_pairs={{0,32},{16,48},{32,0},{48,16},{64,96},{80,112},{96,64},{112,80},{1... | collective-permute-start | bytes 1327112 | tf_op jit(solution)/shard_map/ppermute | solution.py:20
  677.9 8.3 %collective-permute-start.2 = (bf16[3,64,1152]{2,1,0:T(8,128)(2,1)S(1)}, bf16[3,64,1152]{2,1,0:T(8,128)(2,1)S(1)}, u32[]{:S(2)}, u32[]{:S(2)}) collective-permute-start(bf16[3,64,1152]{2,1,0:T(8,128)(2,1)S(1)} %fusion.49), channel_id=1, source_target_pairs={{0,64},{16,80},{32,96},{48,112},{64,0},{80,16},{96,32},{112,48},{1... | collective-permute-start | bytes 1327112 | tf_op jit(solution)/shard_map/ppermute | solution.py:20
  686.2 2.5 copy-start.12
  686.4 22.4 %collective-permute-start.3 = (bf16[3,64,1152]{2,1,0:T(8,128)(2,1)S(1)}, bf16[3,64,1152]{2,1,0:T(8,128)(2,1)}, u32[]{:S(2)}, u32[]{:S(2)}) collective-permute-start(bf16[3,64,1152]{2,1,0:T(8,128)(2,1)S(1)} %fusion.17), channel_id=1, source_target_pairs={{0,128},{16,144},{32,160},{48,176},{64,192},{80,208},{96,224},{112... | collective-permute-start | bytes 1327112 | tf_op jit(solution)/shard_map/ppermute | solution.py:20
  688.7 22.3 %copy-start.3 = (f32[1,3,64,896]{3,2,1,0:T(8,128)S(1)}, f32[1,3,64,896]{3,2,1,0:T(8,128)}, u32[]{:S(2)}) copy-start(f32[1,3,64,896]{3,2,1,0:T(8,128)} %param.23) | copy-start | bytes 2064388
  710.3 3.4 copy-start.16
  710.3 3.4 copy-start.18
  710.3 3.4 copy-start.20
  (1 other events, 0.7 us)
Sparse Core Ops, SparseCore 0:
  11.3 67.0 all-gather.10
  80.1 98.9 all-gather.6
  181.4 185.1 all-gather.8
  385.8 186.6 all-reduce.2
  577.1 78.7 reduce-scatter.1
  711.1 53.4 all-gather.12
